TPU v7x, 32 devices: a whole 2x2x4 slice. The times are simulated.
32 devices in a mesh: dp: 16 (over z, y, x), mp: 2 (over core).
Axes of the slice: x: 2, y: 2, z: 4, core: 2. Of those that a mesh axis runs over, the one named last changes fastest.
Arguments:
- inputs: bfloat16 [6144, 768], P('dp')
- cotangent: bfloat16 [6144, 768], P('dp'), may hold values from -6 to 6
- lengths: int32 [16, 3], P('dp'), may hold values from 0 to 192, as said below
- masked: int32 [6144], P('dp'), may hold values 0 or 1
- replace_ids: int32 [6144], P('dp'), may hold values from 0 to 15359, as said below
- attention_master: float32 [4, 768, 768], P(None, 'dp', 'mp')
- attention_moment: float32 [4, 768, 768], P(None, 'dp', 'mp'), may hold values from -0.1875 to 0.1875
- attention_square: float32 [4, 768, 768], P(None, 'dp', 'mp'), may hold values from 0.00016276042 to 0.0006510417
- geglu_master: float32 [3, 768, 3072], P(None, 'dp', 'mp')
- geglu_moment: float32 [3, 768, 3072], P(None, 'dp', 'mp'), may hold values from -0.1875 to 0.1875
- geglu_square: float32 [3, 768, 3072], P(None, 'dp', 'mp'), may hold values from 0.00016276042 to 0.0006510417
- embed_master: float32 [15360, 768], P('dp', 'mp'), may hold values from -6 to 6
- embed_moment: float32 [15360, 768], P('dp', 'mp'), may hold values from -0.0008544922 to 0.0008544922
- embed_square: float32 [15360, 768], P('dp', 'mp'), may hold values from 3.1789145e-09 to 1.2715658e-08
- norms_master: float32 [4, 768], replicated
- norms_moment: float32 [4, 768], replicated, may hold values from -0.1875 to 0.1875
- norms_square: float32 [4, 768], replicated, may hold values from 0.00016276042 to 0.0006510417
Outputs:
- output: float32 [6144, 768], P('dp')
- input_grad: float32 [6144, 768], P('dp')
- rms_stats: float32 [3], replicated
- lamb_norms: float32 [2, 12], replicated
- attention_grad: float32 [4, 768, 768], P(None, 'dp', 'mp')
- attention_first: float32 [4, 768, 768], P(None, 'dp', 'mp')
- attention_second: float32 [4, 768, 768], P(None, 'dp', 'mp')
- attention_new: float32 [4, 768, 768], P(None, 'dp', 'mp')
- geglu_grad: float32 [3, 768, 3072], P(None, 'dp', 'mp')
- geglu_first: float32 [3, 768, 3072], P(None, 'dp', 'mp')
- geglu_second: float32 [3, 768, 3072], P(None, 'dp', 'mp')
- geglu_new: float32 [3, 768, 3072], P(None, 'dp', 'mp')
- embed_grad: float32 [15360, 768], P('dp', 'mp')
- embed_first: float32 [15360, 768], P('dp', 'mp')
- embed_second: float32 [15360, 768], P('dp', 'mp')
- embed_new: float32 [15360, 768], P('dp', 'mp')
- norms_grad: float32 [4, 768], replicated
- norms_first: float32 [4, 768], replicated
- norms_second: float32 [4, 768], replicated
- norms_new: float32 [4, 768], replicated
Inputs may be any that keep to these rules, and one draw needn't show every extreme that they name: Row d lists the lengths of the sequences given to device d, zeros after; each sequence has 128 tokens or more; a row sums to at most 384, and some row reaches it with a sequence of 192. `replace_ids`: among the 384 slots of one device, exactly 24 ids fall in each aligned block of 960 table rows.
All inputs are finite; a program needn't handle non-finite values. No bound on the sum of `masked` on one device may be relied on, other than what follows from the above.
Results may differ from a plain program's by a relative error of at most 0.016.
The roundings to bfloat16 on the way count: a program that leaves them out, or rounds other values in their place, can miss the bound.
Values may be sent and summed in bfloat16 or wider, within the bound.
A program may use at most 192 MiB of HBM per device.

v0:
```python
import math
import jax
import jax.numpy as jnp
from jax import lax
from jax.sharding import PartitionSpec as P

HEADS = 12
STEP_COUNT = 6
first_decay = 0.5
second_decay = 0.5
learn_rate = 0.3
matrix_decay = 0.01
adam_epsilon = 1e-06
norm_epsilon = 1e-12
masked_score = -1000000000.0


def cut_along(value, dim, length):
    dims = value.shape
    tiles = value.reshape(*dims[:dim], length, dims[dim] // length, *dims[dim + 1 :])
    return jnp.moveaxis(tiles, dim, 0)


def sent_and_summed(value, axis, dim):
    length = lax.axis_size(axis)
    tiles = lax.all_to_all(cut_along(value, dim, length), axis, 0, 0, tiled=True)
    return jnp.sum(tiles.astype(jnp.float32), axis=0)


def layer_norm(values, gain_row, shift_row):
    center = values - jnp.mean(values, axis=-1, keepdims=True)
    spread = jnp.mean(center * center, axis=-1, keepdims=True)
    return center * lax.rsqrt(spread + norm_epsilon) * gain_row + shift_row


def norm_pair(values, gain_pair):
    return layer_norm(values, gain_pair[0], gain_pair[1])


def lamb_parts(master, moment, square, gradient, decay_rate):
    new_moment = first_decay * moment + (1.0 - first_decay) * gradient
    new_square = second_decay * square + (1.0 - second_decay) * gradient * gradient
    update = (
        new_moment
        / (1.0 - first_decay**STEP_COUNT)
        / (jnp.sqrt(new_square / (1.0 - second_decay**STEP_COUNT)) + adam_epsilon)
        + decay_rate * master
    )
    return (new_moment, new_square, update)


def gelu_tanh(values):
    return jax.nn.gelu(values, approximate=True)


def local(
    inputs,
    cotangent,
    lengths,
    masked,
    replace_ids,
    attention_master,
    attention_moment,
    attention_square,
    geglu_master,
    geglu_moment,
    geglu_square,
    embed_master,
    embed_moment,
    embed_square,
    norms_master,
    norms_moment,
    norms_square,
):
    half_type = jnp.bfloat16
    full_type = jnp.float32
    tokens_here = inputs.shape[0]
    width = inputs.shape[1]
    head_dim = width // HEADS
    local_heads = HEADS // lax.axis_size("mp")
    block_len = min(tokens_here, 512)
    attn_scale = 1.0 / math.sqrt(head_dim)
    column_count = embed_master.shape[1]
    attn_low, geglu_low = (
        lax.all_gather(attention_master.astype(half_type), "dp", axis=1, tiled=True),
        lax.all_gather(geglu_master.astype(half_type), "dp", axis=1, tiled=True),
    )
    table_low = lax.all_gather(embed_master.astype(half_type), "dp", axis=0, tiled=True)
    looked_cols = jnp.take(table_low, replace_ids, axis=0)
    looked = lax.all_gather(looked_cols, "mp", axis=1, tiled=True)
    is_masked = masked[:, None] == 1
    hidden_in = jnp.where(is_masked, looked.astype(full_type), inputs.astype(full_type))
    length_row = lengths[0]
    places = jnp.arange(tokens_here, dtype=jnp.int32)
    ends_at = jnp.cumsum(length_row)
    segment_ids = jnp.sum((ends_at[None, :] <= places[:, None]).astype(jnp.int32), axis=1)
    live_rows = (places < jnp.sum(length_row)).astype(full_type)[:, None]
    token_count = jnp.sum(length_row).astype(full_type)
    head_ids = lax.axis_index("mp") * local_heads + jnp.arange(local_heads, dtype=jnp.int32)
    slopes = 2.0 ** (-8.0 * (head_ids.astype(full_type) + 1.0) / HEADS)
    act_low = hidden_in.astype(half_type)
    qkv_low = jnp.einsum(
        "td,kdc->ktc", act_low, attn_low[:3], preferred_element_type=full_type
    ).astype(half_type)
    head_vals = qkv_low.reshape(3, tokens_here, local_heads, head_dim)

    def block_scores(begin_at, query_blk):
        query_pos = begin_at + jnp.arange(block_len, dtype=jnp.int32)
        scores = (
            jnp.einsum("qhe,khe->hqk", query_blk, head_vals[1], preferred_element_type=full_type)
            * attn_scale
        )
        distance = jnp.abs(query_pos[:, None] - places[None, :]).astype(full_type)
        scores = scores - slopes[:, None, None] * distance[None]
        same_seq = segment_ids[:, None] == segment_ids[None, :]
        return jnp.where(same_seq[None], scores, masked_score)

    def forward_block(begin_at):
        query_blk = head_vals[0]
        scores = block_scores(begin_at, query_blk)
        top_score = jnp.max(scores, axis=-1, keepdims=True)
        raised = jnp.exp(scores - top_score)
        row_total = jnp.sum(raised, axis=-1, keepdims=True)
        weights = (raised / row_total).astype(half_type)
        context_blk = jnp.einsum(
            "hqk,khe->qhe", weights, head_vals[2], preferred_element_type=full_type
        )
        return (context_blk.astype(half_type), (top_score + jnp.log(row_total))[..., 0])

    starts = jnp.arange(tokens_here // block_len, dtype=jnp.int32) * block_len
    context_blocks, lse_blocks = lax.map(forward_block, starts)
    context = context_blocks.reshape(tokens_here, local_heads * head_dim)
    attn_part = jnp.einsum("tc,dc->td", context, attn_low[3], preferred_element_type=full_type)
    attn_out = lax.psum(attn_part, "mp")
    normed_one, first_back = jax.vjp(norm_pair, hidden_in + attn_out, norms_master[0:2])
    normed_low = normed_one.astype(half_type)
    gate_up = jnp.einsum("td,kdf->ktf", normed_low, geglu_low[:2], preferred_element_type=full_type)
    gelu_val, gelu_back = jax.vjp(gelu_tanh, gate_up[0])
    inner_act = (gelu_val * gate_up[1]).astype(half_type)
    geglu_part = jnp.einsum("tf,df->td", inner_act, geglu_low[2], preferred_element_type=full_type)
    geglu_out = lax.psum(geglu_part, "mp")
    result, second_back = jax.vjp(norm_pair, normed_one + geglu_out, norms_master[2:4])
    squares = jnp.stack(
        [
            jnp.sum(hidden_in * hidden_in * live_rows),
            jnp.sum(attn_out * attn_out * live_rows),
            jnp.sum(geglu_out * geglu_out * live_rows),
        ]
    )
    count_total, square_total = lax.psum((token_count, squares), "dp")
    rms_stats = jnp.sqrt(square_total / (count_total * width) + 1e-06)
    grad_second, norm_grad_two = second_back(cotangent.astype(full_type) * live_rows)
    grad_geglu = grad_second.astype(half_type)
    grad_inner = jnp.einsum("td,df->tf", grad_geglu, geglu_low[2], preferred_element_type=full_type)
    down_grad = jnp.einsum("td,tf->df", grad_geglu, inner_act, preferred_element_type=full_type)
    grad_gate = gelu_back(grad_inner * gate_up[1])[0]
    grad_up = grad_inner * gelu_val
    grad_gu = jnp.stack([grad_gate, grad_up]).astype(half_type)
    gu_grad = jnp.einsum("td,ktf->kdf", normed_low, grad_gu, preferred_element_type=full_type)
    geglu_local = jnp.concatenate([gu_grad, down_grad[None]], axis=0)
    back_part = jnp.einsum("ktf,kdf->td", grad_gu, geglu_low[:2], preferred_element_type=full_type)
    grad_normed = grad_second + lax.psum(back_part, "mp")
    grad_first_in, norm_grad_one = first_back(grad_normed)
    grad_attn = grad_first_in.astype(half_type)
    grad_context = jnp.einsum(
        "td,dc->tc", grad_attn, attn_low[3], preferred_element_type=full_type
    ).astype(half_type)
    out_grad = jnp.einsum("td,tc->dc", grad_attn, context, preferred_element_type=full_type)
    grad_heads = grad_context.reshape(tokens_here, local_heads, head_dim)

    def backward_block(carry, packed):
        key_acc, value_acc = carry
        begin_at, lse_blk = packed
        query_blk = head_vals[0]
        scores = block_scores(begin_at, query_blk)
        weights = jnp.exp(scores - lse_blk[..., None])
        grad_weights = jnp.einsum(
            "qhe,khe->hqk", grad_heads, head_vals[2], preferred_element_type=full_type
        )
        value_acc = value_acc + jnp.einsum(
            "hqk,qhe->khe", weights.astype(half_type), grad_heads, preferred_element_type=full_type
        )
        row_inner = jnp.sum(grad_weights * weights, axis=-1, keepdims=True)
        grad_scores = (weights * (grad_weights - row_inner)).astype(half_type)
        grad_query = (
            jnp.einsum("hqk,khe->qhe", grad_scores, head_vals[1], preferred_element_type=full_type)
            * attn_scale
        )
        key_acc = (
            key_acc
            + jnp.einsum("hqk,qhe->khe", grad_scores, query_blk, preferred_element_type=full_type)
            * attn_scale
        )
        return ((key_acc, value_acc), grad_query.astype(half_type))

    zero_heads = jnp.zeros((tokens_here, local_heads, head_dim), full_type)
    (key_acc, value_acc), query_grads = lax.scan(
        backward_block, (zero_heads, zero_heads), (starts, lse_blocks)
    )
    grad_qkv = jnp.stack(
        [
            query_grads.reshape(tokens_here, -1),
            key_acc.reshape(tokens_here, -1).astype(half_type),
            value_acc.reshape(tokens_here, -1).astype(half_type),
        ]
    )
    qkv_grad = jnp.einsum("td,ktc->kdc", act_low, grad_qkv, preferred_element_type=full_type)
    act_part = jnp.einsum("ktc,kdc->td", grad_qkv, attn_low[:3], preferred_element_type=full_type)
    grad_in = grad_first_in + lax.psum(act_part.astype(jnp.bfloat16), "mp").astype(jnp.float32)
    input_grad = jnp.where(is_masked, 0.0, grad_in)
    attention_local = jnp.concatenate([qkv_grad, out_grad[None]], axis=0)
    own_columns = lax.dynamic_slice_in_dim(
        grad_in, lax.axis_index("mp") * column_count, column_count, 1
    )
    picked = jnp.where(is_masked, own_columns, 0.0)
    embed_local = jax.ops.segment_sum(picked, replace_ids, num_segments=table_low.shape[0])
    embed_summed = lax.psum_scatter(embed_local, "dp", scatter_dimension=0, tiled=True)
    attention_summed, geglu_summed = (
        sent_and_summed(attention_local.astype(jnp.bfloat16), "dp", 1),
        sent_and_summed(geglu_local.astype(jnp.bfloat16), "dp", 1),
    )
    inverse_count = 1.0 / count_total
    attention_grad = attention_summed * inverse_count
    geglu_grad = geglu_summed * inverse_count
    embed_grad = embed_summed * inverse_count
    attention_first, attention_second, attention_update = lamb_parts(
        attention_master, attention_moment, attention_square, attention_grad, matrix_decay
    )
    geglu_first, geglu_second, geglu_update = lamb_parts(
        geglu_master, geglu_moment, geglu_square, geglu_grad, matrix_decay
    )
    embed_first, embed_second, embed_update = lamb_parts(
        embed_master, embed_moment, embed_square, embed_grad, matrix_decay
    )
    weight_squares = jnp.concatenate(
        [
            jnp.sum(attention_master * attention_master, axis=(1, 2)),
            jnp.sum(geglu_master * geglu_master, axis=(1, 2)),
            jnp.sum(embed_master * embed_master)[None],
        ]
    )
    update_squares = jnp.concatenate(
        [
            jnp.sum(attention_update * attention_update, axis=(1, 2)),
            jnp.sum(geglu_update * geglu_update, axis=(1, 2)),
            jnp.sum(embed_update * embed_update)[None],
        ]
    )
    norms_local = jnp.concatenate([norm_grad_one, norm_grad_two], axis=0)
    weight_total, update_total, norms_summed = lax.psum(
        (weight_squares, update_squares, norms_local * 0.5), ("dp", "mp")
    )
    weight_norms = jnp.sqrt(weight_total)
    update_norms = jnp.sqrt(update_total)
    ratios = weight_norms / update_norms
    attention_new = attention_master - learn_rate * ratios[0:4][:, None, None] * attention_update
    geglu_new = geglu_master - learn_rate * ratios[4:7][:, None, None] * geglu_update
    embed_new = embed_master - learn_rate * ratios[7] * embed_update
    norms_grad = norms_summed * inverse_count
    norms_first, norms_second, norms_update = lamb_parts(
        norms_master, norms_moment, norms_square, norms_grad, 0.0
    )
    norm_weight = jnp.sqrt(jnp.sum(norms_master * norms_master, axis=1))
    norm_update = jnp.sqrt(jnp.sum(norms_update * norms_update, axis=1))
    norms_new = norms_master - learn_rate * (norm_weight / norm_update)[:, None] * norms_update
    lamb_norms = jnp.stack(
        [jnp.concatenate([weight_norms, norm_weight]), jnp.concatenate([update_norms, norm_update])]
    )
    return (
        result,
        input_grad,
        rms_stats,
        lamb_norms,
        attention_grad,
        attention_first,
        attention_second,
        attention_new,
        geglu_grad,
        geglu_first,
        geglu_second,
        geglu_new,
        embed_grad,
        embed_first,
        embed_second,
        embed_new,
        norms_grad,
        norms_first,
        norms_second,
        norms_new,
    )


def solution(mesh):
    in_specs = (
        P("dp", None),
        P("dp", None),
        P("dp", None),
        P("dp"),
        P("dp"),
        P(None, "dp", "mp"),
        P(None, "dp", "mp"),
        P(None, "dp", "mp"),
        P(None, "dp", "mp"),
        P(None, "dp", "mp"),
        P(None, "dp", "mp"),
        P("dp", "mp"),
        P("dp", "mp"),
        P("dp", "mp"),
        P(),
        P(),
        P(),
    )
    out_specs = (
        P("dp", None),
        P("dp", None),
        P(),
        P(),
        P(None, "dp", "mp"),
        P(None, "dp", "mp"),
        P(None, "dp", "mp"),
        P(None, "dp", "mp"),
        P(None, "dp", "mp"),
        P(None, "dp", "mp"),
        P(None, "dp", "mp"),
        P(None, "dp", "mp"),
        P("dp", "mp"),
        P("dp", "mp"),
        P("dp", "mp"),
        P("dp", "mp"),
        P(),
        P(),
        P(),
        P(),
    )
    return jax.shard_map(local, mesh=mesh, in_specs=in_specs, out_specs=out_specs, check_vma=False)
```

profile of v0, /device:TPU:0, one launch (start us, length us, event | category | flops | bytes accessed | tf_op | source)
XLA Modules:
  0.0 1076.4 jit_solution(6731088985889812064)
XLA Ops:
  7.2 1.7 copy.142
  9.1 2.3 convert_element_type.151
  13.5 62.9 %all-gather.6.cloned.1.call-done = bf16[4,768,384]{2,0,1:T(4,128)(2,1)} async-done(((bf16[4,48,384]{2,0,1:T(4,128)(2,1)}), bf16[4,768,384]{2,0,1:T(4,128)(2,1)}) %all-gather.6.cloned.1.call-update) | async-done | bytes 2359312 | tf_op jit(solution)/shard_map/all_gather | solution.py:85
  76.4 5.5 copy.136
  81.9 2.2 slice.94
  84.1 139.1 %all-gather.4.cloned.1.call-done = bf16[15360,384]{1,0:T(8,128)(2,1)} async-done(((bf16[960,384]{1,0:T(8,128)(2,1)}), bf16[15360,384]{1,0:T(8,128)(2,1)}) %all-gather.4.cloned.1.call-update) | async-done | bytes 11796496 | tf_op jit(solution)/shard_map/all_gather | solution.py:88
  223.2 7.9 gather_fusion
  231.2 2.2 all_gather.13
  239.4 1.5 fusion.69
  241.0 2.0 convert_element_type.165
  244.2 14.9 %all-reduce.11.cloned.1.call-done = f32[384,768]{1,0:T(8,128)} async-done(((f32[384,768]{1,0:T(8,128)}), f32[384,768]{1,0:T(8,128)}) %all-reduce.11.cloned.1.call-update) | async-done | bytes 1179664 | tf_op jit(solution)/shard_map/psum | solution.py:134
  259.1 2.0 fusion.92
  262.4 102.8 %all-gather.8.cloned.1.call-done = bf16[3,768,1536]{2,1,0:T(8,128)(2,1)} async-done(((bf16[3,48,1536]{2,1,0:T(8,128)(2,1)}), bf16[3,768,1536]{2,1,0:T(8,128)(2,1)}) %all-gather.8.cloned.1.call-update) | async-done | bytes 7077904 | tf_op jit(solution)/shard_map/all_gather | solution.py:86
  365.1 4.8 fusion.6
  373.1 3.8 fusion.33
  378.9 16.2 %all-reduce.13.cloned.1.call-done = f32[384,768]{1,0:T(8,128)} async-done(((f32[384,768]{1,0:T(8,128)}), f32[384,768]{1,0:T(8,128)}) %all-reduce.13.cloned.1.call-update) | async-done | bytes 1179664 | tf_op jit(solution)/shard_map/psum | solution.py:141
  395.1 2.2 fusion.90
  398.6 1.9 multiply_reduce_fusion.3
  400.6 1.7 fusion.89
  402.2 4.5 fusion.56
  408.3 3.0 fusion.39
  412.3 20.2 %all-reduce.15.cloned.1.call-done = f32[384,768]{1,0:T(8,128)} async-done(((f32[384,768]{1,0:T(8,128)}), f32[384,768]{1,0:T(8,128)}) %all-reduce.15.cloned.1.call-update) | async-done | bytes 1179664 | tf_op jit(solution)/shard_map/psum | solution.py:162
  432.5 4.1 multiply_reduce_fusion.4
  445.4 2.8 fusion.43
  448.2 20.1 %all-reduce.17.cloned.1.call-done = bf16[384,768]{1,0:T(8,128)(2,1)} async-done(((bf16[384,768]{1,0:T(8,128)(2,1)}), bf16[384,768]{1,0:T(8,128)(2,1)}) %all-reduce.17.cloned.1.call-update) | async-done | bytes 589840 | tf_op jit(solution)/shard_map/psum | solution.py:209
  468.4 2.4 broadcast_select_fusion
  470.7 12.5 %scatter_custom_fusion = f32[15360,384]{1,0:T(8,128)} fusion(s32[384]{0:T(512)} %param.21, f32[]{:T(128)} %constant.67.clone.1, f32[384,768]{1,0:T(8,128)S(1)} %get-tuple-element.110, s32[]{:T(128)} %constant.48.clone.1, s32[]{:T(128)S(6)} %select_n.36, pred[384]{0:T(512)(128)(4,1)S(1)} %copy-done.69), kind=kCustom, calls=%fused_computation.3 | custom fusion | flops 294912 | bytes 24184836 | tf_op jit(solution)/shard_map/scatter-add | solution.py:216
  484.6 2.5 convert_bitcast_fusion
  487.1 2.8 copy.118
  491.0 1.8 copy.121
  492.9 6.9 all-to-all-start
  499.9 6.5 convolution_convert_fusion
  507.8 2.6 fusion.10
  510.4 5.8 maximum_bitcast_fusion
  516.2 66.4 %all-to-all-done = bf16[16,4,48,384]{3,2,1,0:T(8,128)(2,1)S(1)} async-done(((bf16[16,4,48,384]{3,2,1,0:T(8,128)(2,1)}), bf16[16,4,48,384]{3,2,1,0:T(8,128)(2,1)S(1)}, u32[]{:S(2)}, u32[]{:S(2)}) %all-to-all-start) | async-done | bytes 2359328 | tf_op jit(solution)/shard_map/all_to_all | solution.py:26
  582.6 29.9 %all-to-all-start.1 = ((bf16[16,3,48,1536]{3,2,1,0:T(8,128)(2,1)}), bf16[16,3,48,1536]{3,2,1,0:T(8,128)(2,1)}, u32[]{:S(2)}, u32[]{:S(2)}) async-start(bf16[16,3,48,1536]{3,2,1,0:T(8,128)(2,1)} %maximum_bitcast_fusion), calls=%async_computation.1 | async-start | bytes 14155776 | tf_op jit(solution)/shard_map/all_to_all | solution.py:26
  613.3 1.9 pad_maximum_fusion.9
  615.2 219.2 %all-reduce.5 = (f32[3]{0:T(128)S(1)}, f32[]{:T(128)}) all-reduce(f32[3]{0:T(128)S(1)} %pad_maximum_fusion.9, f32[]{:T(128)S(6)} %convert_element_type.185), channel_id=1, replica_groups=mesh['dp'=16,'mp'=2] {'dp'}, use_global_device_ids=true, to_apply=%region_21.22 | all-reduce | flops 4 | bytes 32 | tf_op jit(solution)/shard_map/psum | solution.py:150
  837.3 1.7 multiply_reduce_fusion.15
  839.0 4.8 convert_reduce_fusion
  843.8 2.4 multiply_reduce_fusion.13
  846.2 164.9 %reduce-scatter.2.cloned.1.call-done = f32[960,384]{1,0:T(8,128)} async-done(((f32[15360,384]{1,0:T(8,128)}), f32[960,384]{1,0:T(8,128)}) %reduce-scatter.2.cloned.1.call-update) | async-done | bytes 1474576 | tf_op jit(solution)/shard_map/reduce_scatter | solution.py:217
  1011.2 5.4 multiply_reduce_fusion.2
  1016.6 1.9 pad_maximum_fusion.10
  1018.5 39.8 %all-reduce.4 = (f32[4,768]{1,0:T(4,128)}, f32[8]{0:T(128)}, f32[8]{0:T(128)}) all-reduce(f32[4,768]{1,0:T(4,128)} %maximum_multiply_fusion, f32[8]{0:T(128)} %get-tuple-element.142, f32[8]{0:T(128)S(1)} %get-tuple-element.141), channel_id=1, replica_groups=mesh['dp'=16,'mp'=2] {'dp','mp'}, use_global_device_ids=true, to_apply=%region_40.41 | all-reduce | flops 3088 | bytes 24704 | tf_op jit(solution)/shard_map/psum | solution.py:250
  1060.3 1.5 multiply_reduce_fusion.16
  1063.3 1.9 multiply_subtract_fusion.2
  1067.4 1.9 multiply_subtract_fusion
  (251 shorter events, 38.5 us)
Async XLA Ops:
  7.2 69.2 %all-gather.6.cloned.1.call-start = ((), (), s32[]{:S(2)}) async-start(), calls=%async_computation.4 | async-start | bytes 2506752 | tf_op jit(solution)/shard_map/all_gather | solution.py:85
  9.0 214.2 %all-gather.4.cloned.1.call-start = ((), (), s32[]{:S(2)}) async-start(), calls=%async_computation.3 | async-start | bytes 12533760 | tf_op jit(solution)/shard_map/all_gather | solution.py:88
  11.4 247.6 %all-reduce.11.cloned.1.call-start = ((), (), s32[]{:S(2)}) async-start(), calls=%async_computation.5 | async-start | bytes 2359296 | tf_op jit(solution)/shard_map/psum | solution.py:134
  12.7 220.8 %copy-start.67 = (pred[384]{0:T(512)(128)(4,1)}, pred[384]{0:T(512)(128)(4,1)S(1)}, u32[]{:S(2)}) copy-start(pred[384]{0:T(512)(128)(4,1)S(1)} %broadcast_compare_fusion.1) | copy-start | bytes 1156
  76.4 5.5 copy-start.12
  84.1 149.4 %copy-start.23 = (bf16[384,768]{1,0:T(8,128)(2,1)S(1)}, bf16[384,768]{1,0:T(8,128)(2,1)}, u32[]{:S(2)}) copy-start(bf16[384,768]{1,0:T(8,128)(2,1)} %param.17) | copy-start | bytes 1769476
  84.1 149.4 %copy-start.26 = (bf16[3,768,384]{1,2,0:T(8,128)(2,1)S(1)}, bf16[3,768,384]{1,2,0:T(8,128)(2,1)}, u32[]{:S(2)}) copy-start(bf16[3,768,384]{1,2,0:T(8,128)(2,1)} %copy.136) | copy-start | bytes 5308420
  240.9 124.2 %all-gather.8.cloned.1.call-start = ((), (), s32[]{:S(2)}) async-start(), calls=%async_computation.6 | async-start | bytes 7520256 | tf_op jit(solution)/shard_map/all_gather | solution.py:86
  243.0 152.1 %all-reduce.13.cloned.1.call-start = ((), (), s32[]{:S(2)}) async-start(), calls=%async_computation.7 | async-start | bytes 2359296 | tf_op jit(solution)/shard_map/psum | solution.py:141
  261.1 134.0 %copy-start.47 = (f32[384]{0:T(512)}, f32[384]{0:T(512)S(1)}, u32[]{:S(2)}) copy-start(f32[384]{0:T(512)S(1)} %broadcast_multiply_fusion.5) | copy-start | bytes 4612
  262.3 107.6 %copy-start.59 = (f32[384]{0:T(512)}, f32[384]{0:T(512)S(1)}, u32[]{:S(2)}) copy-start(f32[384]{0:T(512)S(1)} %multiply_reduce_fusion.11) | copy-start | bytes 4612
  262.4 132.7 %copy-start.53 = (f32[384]{0:T(512)}, f32[384]{0:T(512)S(1)}, u32[]{:S(2)}) copy-start(f32[384]{0:T(512)S(1)} %fusion.74) | copy-start | bytes 4612
  377.0 55.5 %all-reduce.15.cloned.1.call-start = ((), (), s32[]{:S(2)}) async-start(), calls=%async_computation.8 | async-start | bytes 2359296 | tf_op jit(solution)/shard_map/psum | solution.py:162
  378.9 18.7 %copy-start.52 = (f32[768]{0:T(1024)S(1)}, f32[768]{0:T(1024)}, u32[]{:S(2)}) copy-start(f32[768]{0:T(1024)} %get-tuple-element.83) | copy-start | bytes 9220
  397.3 4.9 slice-start
  400.5 7.7 slice-start.2
  402.2 4.5 copy-start.17
  402.2 4.6 copy-start.70
  402.2 6.1 slice-start.3
  411.4 57.0 %all-reduce.17.cloned.1.call-start = ((), (), s32[]{:S(2)}) async-start(), calls=%async_computation.9 | async-start | bytes 1179648 | tf_op jit(solution)/shard_map/psum | solution.py:209
  445.3 23.0 %copy-start.5 = (f32[384,768]{1,0:T(8,128)S(1)}, f32[384,768]{1,0:T(8,128)}, u32[]{:S(2)}) copy-start(f32[384,768]{1,0:T(8,128)} %copy-done.4) | copy-start | bytes 3538948
  445.3 23.0 %copy-start.58 = (f32[384]{0:T(512)S(1)}, f32[384]{0:T(512)}, u32[]{:S(2)}) copy-start(f32[384]{0:T(512)} %copy-done.57) | copy-start | bytes 4612
  445.3 23.0 %copy-start.69 = (pred[384]{0:T(512)(128)(4,1)S(1)}, pred[384]{0:T(512)(128)(4,1)}, u32[]{:S(2)}) copy-start(pred[384]{0:T(512)(128)(4,1)} %copy-done.67) | copy-start | bytes 1156
  448.2 563.0 %reduce-scatter.2.cloned.1.call-start = ((), (), s32[]{:S(2)}) async-start(), calls=%async_computation.10 | async-start | bytes 25067520 | tf_op jit(solution)/shard_map/reduce_scatter | solution.py:217
  492.9 6.9 copy-start.2
  492.9 6.9 copy-start.49
  492.9 7.0 copy-start.55
  492.9 7.0 copy-start.64
  492.9 89.7 %all-to-all-start = ((bf16[16,4,48,384]{3,2,1,0:T(8,128)(2,1)}), bf16[16,4,48,384]{3,2,1,0:T(8,128)(2,1)S(1)}, u32[]{:S(2)}, u32[]{:S(2)}) async-start(bf16[16,4,48,384]{3,2,1,0:T(8,128)(2,1)} %copy.121), calls=%async_computation | async-start | bytes 4718592 | tf_op jit(solution)/shard_map/all_to_all | solution.py:26
  516.2 318.2 %copy-start.66 = (f32[768]{0:T(1024)S(1)}, f32[768]{0:T(1024)}, u32[]{:S(2)}) copy-start(f32[768]{0:T(1024)} %get-tuple-element.73) | copy-start | bytes 9220
  516.2 319.5 %copy-start.65 = (f32[768]{0:T(1024)S(1)}, f32[768]{0:T(1024)}, u32[]{:S(2)}) copy-start(f32[768]{0:T(1024)} %get-tuple-element.80) | copy-start | bytes 9220
  516.2 320.1 %copy-start.63 = (f32[768]{0:T(1024)S(1)}, f32[768]{0:T(1024)}, u32[]{:S(2)}) copy-start(f32[768]{0:T(1024)} %get-tuple-element.71) | copy-start | bytes 9220
  516.2 320.1 %copy-start.62 = (f32[768]{0:T(1024)S(1)}, f32[768]{0:T(1024)}, u32[]{:S(2)}) copy-start(f32[768]{0:T(1024)} %get-tuple-element.77) | copy-start | bytes 9220
  582.6 256.3 %all-to-all-start.1 = ((bf16[16,3,48,1536]{3,2,1,0:T(8,128)(2,1)}), bf16[16,3,48,1536]{3,2,1,0:T(8,128)(2,1)}, u32[]{:S(2)}, u32[]{:S(2)}) async-start(bf16[16,3,48,1536]{3,2,1,0:T(8,128)(2,1)} %maximum_bitcast_fusion), calls=%async_computation.1 | async-start | bytes 14155776 | tf_op jit(solution)/shard_map/all_to_all | solution.py:26
  612.6 224.7 %copy-start.21 = (f32[4,48,384]{2,1,0:T(8,128)S(1)}, f32[4,48,384]{2,1,0:T(8,128)}, u32[]{:S(2)}) copy-start(f32[4,48,384]{2,1,0:T(8,128)} %param.22) | copy-start | bytes 884740
  612.6 224.7 %copy-start.42 = (f32[4,48,384]{2,1,0:T(8,128)S(1)}, f32[4,48,384]{2,1,0:T(8,128)}, u32[]{:S(2)}) copy-start(f32[4,48,384]{2,1,0:T(8,128)} %param.23) | copy-start | bytes 884740
  612.6 224.7 %copy-start.43 = (f32[4,48,384]{2,1,0:T(8,128)S(1)}, f32[4,48,384]{2,1,0:T(8,128)}, u32[]{:S(2)}) copy-start(f32[4,48,384]{2,1,0:T(8,128)} %param.24) | copy-start | bytes 884740
  839.0 4.8 copy-start.6
  839.0 4.8 copy-start.38
  839.0 4.8 copy-start.39
  843.8 167.4 %copy-start.3 = (f32[960,384]{1,0:T(8,128)S(1)}, f32[960,384]{1,0:T(8,128)}, u32[]{:S(2)}) copy-start(f32[960,384]{1,0:T(8,128)} %param.28) | copy-start | bytes 4423684
  846.2 219.0 %copy-start.19 = (f32[3,48,1536]{2,1,0:T(8,128)}, f32[3,48,1536]{2,1,0:T(8,128)S(1)}, u32[]{:S(2)}) copy-start(f32[3,48,1536]{2,1,0:T(8,128)S(1)} %get-tuple-element.103) | copy-start | bytes 2654212
  846.2 214.1 %copy-start.46 = (f32[4,768]{1,0:T(4,128)S(1)}, f32[4,768]{1,0:T(4,128)}, u32[]{:S(2)}) copy-start(f32[4,768]{1,0:T(4,128)} %param.31) | copy-start | bytes 36868
  1011.2 5.4 copy-start.73
  1011.2 5.4 copy-start.74
  1011.2 5.4 copy-start.75
  1011.2 5.4 copy-start.76
  1058.3 7.0 copy-start.20
  (47 other events, 95.2 us)
Sparse Core Ops, SparseCore 0:
  11.4 64.9 all-gather.5
  79.8 143.3 all-gather.3
  241.1 17.9 all-reduce.10
  262.6 102.5 all-gather.7
  377.1 17.9 all-reduce.12
  411.5 20.9 all-reduce.14
  448.3 20.0 all-reduce.16
  483.5 527.6 reduce-scatter.1
where the time goes:
time: 1080 us
  waiting for transfers between devices  608 us (56%)
  blocking collectives  261 us (24%)
  other arithmetic  73.6 us (7%)
  matrix products  39.9 us (4%)
  local copies, waits for them, and re-layouts  38.1 us (4%)
  starting transfers between devices  37.9 us (4%)
  between operations  18.1 us (2%)
    psum x1, blocking collectives, local(): count_total, square_total = lax.psum((token_count, squares), 'dp')  219 us
    reduce_scatter x1, waiting for transfers between devices, local(): lax.psum_scatter(embed_local, 'dp', scatter_dimension=0, tiled=True)  165 us
    all_gather x1, waiting for transfers between devices, local(): lax.all_gather(embed_master.astype(half_type), 'dp', axis=0, tiled=True)  139 us
    all_gather x1, waiting for transfers between devices, local(): lax.all_gather(geglu_master.astype(half_type), 'dp', axis=1, tiled=True)  103 us
    all_to_all x2, waiting for transfers between devices, sent_and_summed(): lax.all_to_all(cut_along(value, dim, length), axis, 0, 0, tiled=True)  66.4 us
    all_gather x1, waiting for transfers between devices, local(): lax.all_gather(attention_master.astype(half_type), 'dp', axis=1, tiled=True)  62.9 us
    psum x1, blocking collectives, local(): lax.psum((weight_squares, update_squares, norms_local * 0.5), ('dp', 'mp'))  39.8 us
    all_to_all x2, starting transfers between devices, sent_and_summed(): lax.all_to_all(cut_along(value, dim, length), axis, 0, 0, tiled=True)  36.9 us
  transfers between devices with their start and end apart: 10, of which 9 were waited for; matrix products, arithmetic and copies ran while one was open for 5% of the time, Pallas kernels for 0%

commit v1 on v0

--- a/solution.py
+++ b/solution.py
@@ -247,8 +247,13 @@
         ]
     )
     norms_local = jnp.concatenate([norm_grad_one, norm_grad_two], axis=0)
-    weight_total, update_total, norms_summed = lax.psum(
-        (weight_squares, update_squares, norms_local * 0.5), ("dp", "mp")
+
+    def number_the_region(inner_x):
+        value_now = jax.lax.psum(jax.lax.psum(inner_x, axis_name="mp"), axis_name="dp")
+        return value_now
+
+    weight_total, update_total, norms_summed = number_the_region(
+        (weight_squares, update_squares, norms_local * 0.5)
     )
     weight_norms = jnp.sqrt(weight_total)
     update_norms = jnp.sqrt(update_total)

time: 1080 us -> 1130 us (1.046)
  blocking collectives: 261 us -> 303 us
    psum x1 -> x2, blocking collectives: 219 us -> 296 us  [local(): count_total, square_total = lax.psum((token_count, squares), 'dp')]
    psum x1, blocking collectives: 39.8 us -> 4.57 us  [number_the_region(): jax.lax.psum(inner_x, axis_name='mp')]
where the time goes in v1:
time: 1130 us; the launch traced here: 1120 us
  waiting for transfers between devices  606 us (54%)
  blocking collectives  303 us (27%)
  other arithmetic  74.3 us (7%)
  matrix products  39.9 us (4%)
  local copies, waits for them, and re-layouts  38.1 us (3%)
  starting transfers between devices  37.9 us (3%)
  between operations  18.2 us (2%)
    psum x2, blocking collectives, local(): count_total, square_total = lax.psum((token_count, squares), 'dp')  296 us
    reduce_scatter x1, waiting for transfers between devices, local(): lax.psum_scatter(embed_local, 'dp', scatter_dimension=0, tiled=True)  163 us
    all_gather x1, waiting for transfers between devices, local(): lax.all_gather(embed_master.astype(half_type), 'dp', axis=0, tiled=True)  139 us
    all_gather x1, waiting for transfers between devices, local(): lax.all_gather(geglu_master.astype(half_type), 'dp', axis=1, tiled=True)  103 us
    all_to_all x2, waiting for transfers between devices, sent_and_summed(): lax.all_to_all(cut_along(value, dim, length), axis, 0, 0, tiled=True)  66.4 us
    all_gather x1, waiting for transfers between devices, local(): lax.all_gather(attention_master.astype(half_type), 'dp', axis=1, tiled=True)  62.9 us
    all_to_all x2, starting transfers between devices, sent_and_summed(): lax.all_to_all(cut_along(value, dim, length), axis, 0, 0, tiled=True)  36.9 us
  transfers between devices with their start and end apart: 10, of which 9 were waited for; matrix products, arithmetic and copies ran while one was open for 5% of the time, Pallas kernels for 0%

profile of v1, /device:TPU:0, one launch (start us, length us, event | category | flops | bytes accessed | tf_op | source)
XLA Modules:
  0.0 1117.3 jit_solution(4738766813360312366)
XLA Ops:
  7.2 1.7 copy.142
  9.1 2.3 convert_element_type.151
  13.5 62.9 %all-gather.6.cloned.1.call-done = bf16[4,768,384]{2,0,1:T(4,128)(2,1)} async-done(((bf16[4,48,384]{2,0,1:T(4,128)(2,1)}), bf16[4,768,384]{2,0,1:T(4,128)(2,1)}) %all-gather.6.cloned.1.call-update) | async-done | bytes 2359312 | tf_op jit(solution)/shard_map/all_gather | solution.py:85
  76.4 5.4 copy.136
  81.9 2.2 slice.94
  84.1 139.1 %all-gather.4.cloned.1.call-done = bf16[15360,384]{1,0:T(8,128)(2,1)} async-done(((bf16[960,384]{1,0:T(8,128)(2,1)}), bf16[15360,384]{1,0:T(8,128)(2,1)}) %all-gather.4.cloned.1.call-update) | async-done | bytes 11796496 | tf_op jit(solution)/shard_map/all_gather | solution.py:88
  223.2 7.9 gather_fusion
  231.2 2.2 all_gather.13
  239.4 1.5 fusion.69
  241.0 2.0 convert_element_type.165
  244.2 14.9 %all-reduce.11.cloned.1.call-done = f32[384,768]{1,0:T(8,128)} async-done(((f32[384,768]{1,0:T(8,128)}), f32[384,768]{1,0:T(8,128)}) %all-reduce.11.cloned.1.call-update) | async-done | bytes 1179664 | tf_op jit(solution)/shard_map/psum | solution.py:134
  259.1 2.0 fusion.92
  262.4 102.8 %all-gather.8.cloned.1.call-done = bf16[3,768,1536]{2,1,0:T(8,128)(2,1)} async-done(((bf16[3,48,1536]{2,1,0:T(8,128)(2,1)}), bf16[3,768,1536]{2,1,0:T(8,128)(2,1)}) %all-gather.8.cloned.1.call-update) | async-done | bytes 7077904 | tf_op jit(solution)/shard_map/all_gather | solution.py:86
  365.1 4.8 fusion.6
  373.1 3.8 fusion.33
  378.9 16.2 %all-reduce.13.cloned.1.call-done = f32[384,768]{1,0:T(8,128)} async-done(((f32[384,768]{1,0:T(8,128)}), f32[384,768]{1,0:T(8,128)}) %all-reduce.13.cloned.1.call-update) | async-done | bytes 1179664 | tf_op jit(solution)/shard_map/psum | solution.py:141
  395.1 2.2 fusion.90
  398.6 1.9 multiply_reduce_fusion.3
  400.6 1.7 fusion.89
  402.3 4.5 fusion.56
  408.3 3.0 fusion.39
  412.3 20.2 %all-reduce.15.cloned.1.call-done = f32[384,768]{1,0:T(8,128)} async-done(((f32[384,768]{1,0:T(8,128)}), f32[384,768]{1,0:T(8,128)}) %all-reduce.15.cloned.1.call-update) | async-done | bytes 1179664 | tf_op jit(solution)/shard_map/psum | solution.py:162
  432.5 4.1 multiply_reduce_fusion.4
  445.4 2.8 fusion.43
  448.3 20.1 %all-reduce.17.cloned.1.call-done = bf16[384,768]{1,0:T(8,128)(2,1)} async-done(((bf16[384,768]{1,0:T(8,128)(2,1)}), bf16[384,768]{1,0:T(8,128)(2,1)}) %all-reduce.17.cloned.1.call-update) | async-done | bytes 589840 | tf_op jit(solution)/shard_map/psum | solution.py:209
  468.4 2.4 broadcast_select_fusion
  470.8 12.5 %scatter_custom_fusion = f32[15360,384]{1,0:T(8,128)} fusion(s32[384]{0:T(512)} %param.21, f32[]{:T(128)} %constant.67.clone.1, f32[384,768]{1,0:T(8,128)S(1)} %get-tuple-element.112, s32[]{:T(128)} %constant.48.clone.1, s32[]{:T(128)S(6)} %select_n.36, pred[384]{0:T(512)(128)(4,1)S(1)} %copy-done.69), kind=kCustom, calls=%fused_computation.3 | custom fusion | flops 294912 | bytes 24184836 | tf_op jit(solution)/shard_map/scatter-add | solution.py:216
  484.6 2.5 convert_bitcast_fusion
  487.1 2.8 copy.118
  491.0 1.8 copy.121
  492.9 6.9 all-to-all-start
  499.8 6.5 convolution_convert_fusion
  507.7 2.7 fusion.10
  510.4 5.8 maximum_bitcast_fusion
  516.2 66.4 %all-to-all-done = bf16[16,4,48,384]{3,2,1,0:T(8,128)(2,1)S(1)} async-done(((bf16[16,4,48,384]{3,2,1,0:T(8,128)(2,1)}), bf16[16,4,48,384]{3,2,1,0:T(8,128)(2,1)S(1)}, u32[]{:S(2)}, u32[]{:S(2)}) %all-to-all-start) | async-done | bytes 2359328 | tf_op jit(solution)/shard_map/all_to_all | solution.py:26
  582.6 29.9 %all-to-all-start.1 = ((bf16[16,3,48,1536]{3,2,1,0:T(8,128)(2,1)}), bf16[16,3,48,1536]{3,2,1,0:T(8,128)(2,1)}, u32[]{:S(2)}, u32[]{:S(2)}) async-start(bf16[16,3,48,1536]{3,2,1,0:T(8,128)(2,1)} %maximum_bitcast_fusion), calls=%async_computation.1 | async-start | bytes 14155776 | tf_op jit(solution)/shard_map/all_to_all | solution.py:26
  613.3 221.6 %psum.89 = f32[]{:T(128)} all-reduce(f32[]{:T(128)S(6)} %convert_element_type.185), channel_id=1, replica_groups=mesh['dp'=16,'mp'=2] {'dp'}, use_global_device_ids=true, to_apply=%region_22.23 | all-reduce | flops 1 | bytes 8 | tf_op jit(solution)/shard_map/psum | solution.py:150
  836.3 2.0 pad_maximum_fusion.9
  839.3 1.7 multiply_reduce_fusion.15
  841.0 4.7 convert_reduce_fusion
  845.7 2.4 multiply_reduce_fusion.13
  848.2 163.1 %reduce-scatter.2.cloned.1.call-done = f32[960,384]{1,0:T(8,128)} async-done(((f32[15360,384]{1,0:T(8,128)}), f32[960,384]{1,0:T(8,128)}) %reduce-scatter.2.cloned.1.call-update) | async-done | bytes 1474576 | tf_op jit(solution)/shard_map/reduce_scatter | solution.py:217
  1011.3 5.4 multiply_reduce_fusion.2
  1016.7 1.9 pad_maximum_fusion.10
  1018.6 4.6 all-reduce.5
  1023.2 74.9 %all-reduce.4 = (f32[3]{0:T(128)}, f32[4,768]{1,0:T(4,128)}, f32[8]{0:T(128)}, f32[8]{0:T(128)}) all-reduce(f32[3]{0:T(128)S(1)} %pad_maximum_fusion.9, f32[4,768]{1,0:T(4,128)} %get-tuple-element.94, f32[8]{0:T(128)} %get-tuple-element.95, f32[8]{0:T(128)} %get-tuple-element.96), channel_id=1, replica_groups=mesh['dp'=16,'mp'=2] {'dp'}, use_global_device_ids=true, to_apply=%region_21.22 | all-reduce | flops 3091 | bytes 24728 | tf_op jit(solution)/shard_map/psum | solution.py:150
  1104.2 1.9 multiply_subtract_fusion.2
  1108.3 1.9 multiply_subtract_fusion
  (252 shorter events, 40.6 us)
Async XLA Ops:
  7.2 69.2 %all-gather.6.cloned.1.call-start = ((), (), s32[]{:S(2)}) async-start(), calls=%async_computation.4 | async-start | bytes 2506752 | tf_op jit(solution)/shard_map/all_gather | solution.py:85
  9.0 214.2 %all-gather.4.cloned.1.call-start = ((), (), s32[]{:S(2)}) async-start(), calls=%async_computation.3 | async-start | bytes 12533760 | tf_op jit(solution)/shard_map/all_gather | solution.py:88
  11.4 247.6 %all-reduce.11.cloned.1.call-start = ((), (), s32[]{:S(2)}) async-start(), calls=%async_computation.5 | async-start | bytes 2359296 | tf_op jit(solution)/shard_map/psum | solution.py:134
  12.7 220.8 %copy-start.67 = (pred[384]{0:T(512)(128)(4,1)}, pred[384]{0:T(512)(128)(4,1)S(1)}, u32[]{:S(2)}) copy-start(pred[384]{0:T(512)(128)(4,1)S(1)} %broadcast_compare_fusion.1) | copy-start | bytes 1156
  76.4 5.4 copy-start.12
  84.1 149.4 %copy-start.23 = (bf16[384,768]{1,0:T(8,128)(2,1)S(1)}, bf16[384,768]{1,0:T(8,128)(2,1)}, u32[]{:S(2)}) copy-start(bf16[384,768]{1,0:T(8,128)(2,1)} %param.17) | copy-start | bytes 1769476
  84.1 149.4 %copy-start.26 = (bf16[3,768,384]{1,2,0:T(8,128)(2,1)S(1)}, bf16[3,768,384]{1,2,0:T(8,128)(2,1)}, u32[]{:S(2)}) copy-start(bf16[3,768,384]{1,2,0:T(8,128)(2,1)} %copy.136) | copy-start | bytes 5308420
  240.9 124.2 %all-gather.8.cloned.1.call-start = ((), (), s32[]{:S(2)}) async-start(), calls=%async_computation.6 | async-start | bytes 7520256 | tf_op jit(solution)/shard_map/all_gather | solution.py:86
  243.0 152.1 %all-reduce.13.cloned.1.call-start = ((), (), s32[]{:S(2)}) async-start(), calls=%async_computation.7 | async-start | bytes 2359296 | tf_op jit(solution)/shard_map/psum | solution.py:141
  261.1 134.0 %copy-start.47 = (f32[384]{0:T(512)}, f32[384]{0:T(512)S(1)}, u32[]{:S(2)}) copy-start(f32[384]{0:T(512)S(1)} %broadcast_multiply_fusion.5) | copy-start | bytes 4612
  262.3 107.6 %copy-start.59 = (f32[384]{0:T(512)}, f32[384]{0:T(512)S(1)}, u32[]{:S(2)}) copy-start(f32[384]{0:T(512)S(1)} %multiply_reduce_fusion.11) | copy-start | bytes 4612
  262.4 132.7 %copy-start.53 = (f32[384]{0:T(512)}, f32[384]{0:T(512)S(1)}, u32[]{:S(2)}) copy-start(f32[384]{0:T(512)S(1)} %fusion.74) | copy-start | bytes 4612
  377.0 55.5 %all-reduce.15.cloned.1.call-start = ((), (), s32[]{:S(2)}) async-start(), calls=%async_computation.8 | async-start | bytes 2359296 | tf_op jit(solution)/shard_map/psum | solution.py:162
  378.9 18.7 %copy-start.52 = (f32[768]{0:T(1024)S(1)}, f32[768]{0:T(1024)}, u32[]{:S(2)}) copy-start(f32[768]{0:T(1024)} %get-tuple-element.83) | copy-start | bytes 9220
  397.3 4.9 slice-start
  400.6 7.7 slice-start.2
  402.2 4.6 copy-start.17
  402.3 4.6 copy-start.70
  402.3 6.0 slice-start.3
  411.4 57.0 %all-reduce.17.cloned.1.call-start = ((), (), s32[]{:S(2)}) async-start(), calls=%async_computation.9 | async-start | bytes 1179648 | tf_op jit(solution)/shard_map/psum | solution.py:209
  445.4 23.0 %copy-start.5 = (f32[384,768]{1,0:T(8,128)S(1)}, f32[384,768]{1,0:T(8,128)}, u32[]{:S(2)}) copy-start(f32[384,768]{1,0:T(8,128)} %copy-done.4) | copy-start | bytes 3538948
  445.4 23.0 %copy-start.58 = (f32[384]{0:T(512)S(1)}, f32[384]{0:T(512)}, u32[]{:S(2)}) copy-start(f32[384]{0:T(512)} %copy-done.57) | copy-start | bytes 4612
  445.4 23.0 %copy-start.69 = (pred[384]{0:T(512)(128)(4,1)S(1)}, pred[384]{0:T(512)(128)(4,1)}, u32[]{:S(2)}) copy-start(pred[384]{0:T(512)(128)(4,1)} %copy-done.67) | copy-start | bytes 1156
  448.2 563.0 %reduce-scatter.2.cloned.1.call-start = ((), (), s32[]{:S(2)}) async-start(), calls=%async_computation.10 | async-start | bytes 25067520 | tf_op jit(solution)/shard_map/reduce_scatter | solution.py:217
  492.9 6.9 copy-start.2
  492.9 6.9 copy-start.49
  492.9 7.0 copy-start.55
  492.9 7.0 copy-start.64
  492.9 89.7 %all-to-all-start = ((bf16[16,4,48,384]{3,2,1,0:T(8,128)(2,1)}), bf16[16,4,48,384]{3,2,1,0:T(8,128)(2,1)S(1)}, u32[]{:S(2)}, u32[]{:S(2)}) async-start(bf16[16,4,48,384]{3,2,1,0:T(8,128)(2,1)} %copy.121), calls=%async_computation | async-start | bytes 4718592 | tf_op jit(solution)/shard_map/all_to_all | solution.py:26
  516.2 320.1 %copy-start.66 = (f32[768]{0:T(1024)S(1)}, f32[768]{0:T(1024)}, u32[]{:S(2)}) copy-start(f32[768]{0:T(1024)} %get-tuple-element.73) | copy-start | bytes 9220
  516.2 320.1 %copy-start.65 = (f32[768]{0:T(1024)S(1)}, f32[768]{0:T(1024)}, u32[]{:S(2)}) copy-start(f32[768]{0:T(1024)} %get-tuple-element.80) | copy-start | bytes 9220
  516.2 322.1 %copy-start.63 = (f32[768]{0:T(1024)S(1)}, f32[768]{0:T(1024)}, u32[]{:S(2)}) copy-start(f32[768]{0:T(1024)} %get-tuple-element.71) | copy-start | bytes 9220
  516.2 322.1 %copy-start.62 = (f32[768]{0:T(1024)S(1)}, f32[768]{0:T(1024)}, u32[]{:S(2)}) copy-start(f32[768]{0:T(1024)} %get-tuple-element.77) | copy-start | bytes 9220
  582.6 258.4 %all-to-all-start.1 = ((bf16[16,3,48,1536]{3,2,1,0:T(8,128)(2,1)}), bf16[16,3,48,1536]{3,2,1,0:T(8,128)(2,1)}, u32[]{:S(2)}, u32[]{:S(2)}) async-start(bf16[16,3,48,1536]{3,2,1,0:T(8,128)(2,1)} %maximum_bitcast_fusion), calls=%async_computation.1 | async-start | bytes 14155776 | tf_op jit(solution)/shard_map/all_to_all | solution.py:26
  612.6 226.7 %copy-start.21 = (f32[4,48,384]{2,1,0:T(8,128)S(1)}, f32[4,48,384]{2,1,0:T(8,128)}, u32[]{:S(2)}) copy-start(f32[4,48,384]{2,1,0:T(8,128)} %param.22) | copy-start | bytes 884740
  612.6 226.7 %copy-start.42 = (f32[4,48,384]{2,1,0:T(8,128)S(1)}, f32[4,48,384]{2,1,0:T(8,128)}, u32[]{:S(2)}) copy-start(f32[4,48,384]{2,1,0:T(8,128)} %param.23) | copy-start | bytes 884740
  612.6 226.7 %copy-start.43 = (f32[4,48,384]{2,1,0:T(8,128)S(1)}, f32[4,48,384]{2,1,0:T(8,128)}, u32[]{:S(2)}) copy-start(f32[4,48,384]{2,1,0:T(8,128)} %param.24) | copy-start | bytes 884740
  841.0 4.7 copy-start.6
  841.0 4.7 copy-start.38
  841.0 4.7 copy-start.39
  845.7 165.5 %copy-start.3 = (f32[960,384]{1,0:T(8,128)S(1)}, f32[960,384]{1,0:T(8,128)}, u32[]{:S(2)}) copy-start(f32[960,384]{1,0:T(8,128)} %param.28) | copy-start | bytes 4423684
  848.2 258.0 %copy-start.19 = (f32[3,48,1536]{2,1,0:T(8,128)}, f32[3,48,1536]{2,1,0:T(8,128)S(1)}, u32[]{:S(2)}) copy-start(f32[3,48,1536]{2,1,0:T(8,128)S(1)} %get-tuple-element.105) | copy-start | bytes 2654212
  848.2 253.1 %copy-start.46 = (f32[4,768]{1,0:T(4,128)S(1)}, f32[4,768]{1,0:T(4,128)}, u32[]{:S(2)}) copy-start(f32[4,768]{1,0:T(4,128)} %param.31) | copy-start | bytes 36868
  1011.2 5.4 copy-start.73
  1011.2 5.4 copy-start.74
  1011.3 5.4 copy-start.75
  1011.3 5.4 copy-start.76
  1098.0 8.1 copy-start.20
  (47 other events, 95.3 us)
Sparse Core Ops, SparseCore 0:
  11.4 64.9 all-gather.5
  79.8 143.3 all-gather.3
  241.1 17.9 all-reduce.10
  262.6 102.5 all-gather.7
  377.1 17.9 all-reduce.12
  411.5 20.9 all-reduce.14
  448.3 20.0 all-reduce.16
  483.5 527.7 reduce-scatter.1
